TPU v7x, 32 devices: a whole 2x2x4 slice. The times are simulated.
32 devices in a mesh: group: 2 (over y), dp: 4 (over x, core), seq: 4 (over z).
Axes of the slice: x: 2, y: 2, z: 4, core: 2. Of those that a mesh axis runs over, the one named last changes fastest.
Arguments:
- tokens: bfloat16 [8, 1024, 4096], P(('group', 'dp'), 'seq'), parts along dimension 0, may hold values from -6 to 6
- norm_gain: bfloat16 [4096], replicated, may hold values from 0.099609375 to 1.8984375
- qkv_weight: bfloat16 [4096, 3072], P('dp'), may hold values from -4 to 4, as said below
- doc_ids: int32 [8, 1024], P(('group', 'dp'), 'seq'), parts along dimension 0, may hold values from 0 to 5, never falling along the last dimension, each value on 1 to 512 neighbouring positions
Outputs:
- attended: bfloat16 [8, 1024, 2048], P(('group', 'dp'), 'seq'), parts along dimension 0
There are 2 independent parts, one for each index of `group`. A program takes and returns all parts, laid end to end along the dimension named above; an argument that names none is the same for every part. Nothing has to cross between parts.
Inputs may be any that keep to these rules, and one draw needn't show every extreme that they name: `qkv_weight`: in the hidden draw query heads lie close to multiples of their key head. `doc_ids`: ids never fall along a sequence; a document holds at most 512 positions.
All inputs are finite; a program needn't handle non-finite values.
Results may differ from a plain program's by a relative error of at most 0.0075.
Values may be sent and summed in bfloat16 or wider, within the bound.
No kernel may reach another device: no remote copies, remote signals or barrier semaphores. Data moves between devices by JAX's collectives and lax.ppermute only.
A program may use at most 128 MiB of HBM per device.

v0:
```python
import jax
import jax.numpy as jnp
from jax import lax
from jax.sharding import PartitionSpec as P

HD = 128
QH = 16
KVH = 4
QW = 2048
KW = 512


def rms_norm(rows, gain):
    values = rows.astype(jnp.float32)
    scale = lax.rsqrt(jnp.mean(values * values, axis=-1, keepdims=True) + 1e-05)
    return (values * scale * gain.astype(jnp.float32)).astype(jnp.bfloat16)


def rotate(heads, places):
    half = heads.shape[-1] // 2
    freqs = 500000.0 ** (-2.0 * jnp.arange(half, dtype=jnp.float32) / heads.shape[-1])
    angles = places[:, None] * freqs[None, :]
    cosine = jnp.cos(angles)[:, None, :]
    sine = jnp.sin(angles)[:, None, :]
    first = heads[..., :half]
    second = heads[..., half:]
    return jnp.concatenate(
        [first * cosine - second * sine, second * cosine + first * sine], axis=-1
    )


def attend(queries, keys, values, docs):
    length = queries.shape[0]
    local_q = queries.shape[1]
    local_kv = keys.shape[1]
    share = local_q // local_kv
    queries = queries.reshape(length, local_kv, share, HD)
    block = min(512, length)
    scale = 1.0 / HD**0.5
    cols = jnp.arange(length, dtype=jnp.int32)

    def one_block(index):
        start = index * block
        qblock = lax.dynamic_slice_in_dim(queries, start, block, 0)
        scores = (
            jnp.einsum("qkgd,tkd->kgqt", qblock, keys, preferred_element_type=jnp.float32) * scale
        )
        rowpos = start + jnp.arange(block, dtype=jnp.int32)
        rowdoc = lax.dynamic_slice_in_dim(docs, start, block, 0)
        allow = (cols[None, :] <= rowpos[:, None]) & (docs[None, :] == rowdoc[:, None])
        scores = jnp.where(allow[None, None], scores, -1e30)
        peak = jnp.max(scores, axis=-1, keepdims=True)
        expo = jnp.where(allow[None, None], jnp.exp(scores - peak), 0.0)
        total = jnp.sum(expo, axis=-1)
        weights = expo.astype(jnp.bfloat16)
        outs = jnp.einsum("kgqt,tkd->qkgd", weights, values, preferred_element_type=jnp.float32)
        outs = outs / jnp.transpose(total, (2, 0, 1))[..., None]
        return outs.reshape(block, local_q * HD).astype(jnp.bfloat16)

    result = lax.map(one_block, jnp.arange(length // block, dtype=jnp.int32))
    return result.reshape(length, local_q * HD)


def local(tokens, norm_gain, qkv_weight, doc_ids):
    count = lax.axis_size("seq")
    rank = lax.axis_index("seq")
    tok = tokens.shape[1]
    length = tok * count
    local_q = QH // count
    normed = rms_norm(tokens[0], norm_gain)
    all_docs = lax.all_gather(doc_ids, "seq", axis=1, tiled=True)[0]
    proj = jnp.dot(
        normed,
        lax.all_gather(qkv_weight, "dp", axis=0, tiled=True),
        preferred_element_type=jnp.float32,
    )
    places = (rank * tok + jnp.arange(tok, dtype=jnp.int32)).astype(jnp.float32)
    queries = rotate(proj[:, :QW].reshape(tok, QH, HD), places).astype(jnp.bfloat16)
    keys = rotate(proj[:, QW : QW + KW].reshape(tok, KVH, HD), places).astype(jnp.bfloat16)
    values = proj[:, QW + KW :].reshape(tok, KVH, HD).astype(jnp.bfloat16)
    slots = max(KVH, count)
    if slots > KVH:
        keys = jnp.repeat(keys, slots // KVH, axis=1)
        values = jnp.repeat(values, slots // KVH, axis=1)
    q_sent = queries.reshape(tok, count, local_q * HD)
    q_got, k_got, v_got = (
        lax.all_to_all(q_sent, "seq", split_axis=1, concat_axis=0, tiled=True),
        lax.all_to_all(keys, "seq", split_axis=1, concat_axis=0, tiled=True),
        lax.all_to_all(values, "seq", split_axis=1, concat_axis=0, tiled=True),
    )
    q_heads = q_got.reshape(length, local_q, HD)
    outputs = attend(q_heads, k_got, v_got, all_docs)
    back = outputs.reshape(count, tok, local_q * HD)
    return lax.all_to_all(back, "seq", split_axis=0, concat_axis=2, tiled=True)


def solution(mesh):
    in_specs = (P(("group", "dp"), "seq", None), P(), P("dp", None), P(("group", "dp"), "seq"))
    out_specs = P(("group", "dp"), "seq", None)
    return jax.shard_map(local, mesh=mesh, in_specs=in_specs, out_specs=out_specs, check_vma=False)
```

profile of v0, /device:TPU:0, one launch (start us, length us, event | category | flops | bytes accessed | tf_op | source)
XLA Modules:
  0.0 297.0 jit_solution(6609023048014826242)
XLA Ops:
  7.3 0.8 copy-done.1
  9.0 157.5 %all-gather.2.cloned.1.call-done = bf16[4096,3072]{1,0:T(8,128)(2,1)} async-done(((bf16[1024,3072]{1,0:T(8,128)(2,1)}), bf16[4096,3072]{1,0:T(8,128)(2,1)}) %all-gather.2.cloned.1.call-update) | async-done | bytes 25165840 | tf_op jit(solution)/shard_map/all_gather | solution.py:74
  166.4 11.6 %fusion.24 = f32[256,3072]{1,0:T(8,128)S(1)} fusion(bf16[4096,3072]{1,0:T(8,128)(2,1)} %all-gather.2.cloned.1.call-done, bf16[1,256,4096]{2,1,0:T(8,128)(2,1)S(1)} %copy-done.1, f32[4096]{0:T(1024)S(1)} %convert_element_type.47, f32[256]{0:T(256)S(1)} %add_rsqrt_fusion), kind=kOutput, calls=%fused_computation.28 | convolution fusion | flops 6446645248 | bytes 30426112 | tf_op jit(solution)/shard_map/dot_general | solution.py:72
  178.1 1.6 slice.29
  180.4 0.8 copy_bitcast_fusion.2
  181.2 2.0 copy.35
  183.2 4.6 %all-to-all-start.2 = ((bf16[256,4,128]{2,0,1:T(8,128)(2,1)}), bf16[256,4,128]{2,0,1:T(8,128)(2,1)S(1)}, u32[]{:S(2)}, u32[]{:S(2)}) async-start(bf16[256,4,128]{2,0,1:T(8,128)(2,1)} %copy_bitcast_fusion.2), calls=%async_computation.2 | async-start | bytes 524288 | tf_op jit(solution)/shard_map/all_to_all | solution.py:89
  188.1 1.1 pad_maximum_fusion
  189.2 7.9 %all-to-all-done.2 = bf16[256,4,128]{2,0,1:T(8,128)(2,1)S(1)} async-done(((bf16[256,4,128]{2,0,1:T(8,128)(2,1)}), bf16[256,4,128]{2,0,1:T(8,128)(2,1)S(1)}, u32[]{:S(2)}, u32[]{:S(2)}) %all-to-all-start.2) | async-done | bytes 262176 | tf_op jit(solution)/shard_map/all_to_all | solution.py:89
  197.1 3.5 %all-to-all-start = ((bf16[256,4,512]{0,2,1:T(8,128)(2,1)}), bf16[256,4,512]{0,2,1:T(8,128)(2,1)S(1)}, u32[]{:S(2)}, u32[]{:S(2)}) async-start(bf16[256,4,512]{0,2,1:T(8,128)(2,1)} %bitcast.3), calls=%async_computation | async-start | bytes 2097152 | tf_op jit(solution)/shard_map/all_to_all | solution.py:87
  201.5 0.9 pad_maximum_fusion.1
  202.4 22.4 %all-to-all-done = bf16[256,4,512]{0,2,1:T(8,128)(2,1)S(1)} async-done(((bf16[256,4,512]{0,2,1:T(8,128)(2,1)}), bf16[256,4,512]{0,2,1:T(8,128)(2,1)S(1)}, u32[]{:S(2)}, u32[]{:S(2)}) %all-to-all-start) | async-done | bytes 1048608 | tf_op jit(solution)/shard_map/all_to_all | solution.py:87
  224.8 3.4 %all-to-all-start.1 = ((bf16[256,4,128]{2,0,1:T(8,128)(2,1)}), bf16[256,4,128]{2,0,1:T(8,128)(2,1)S(1)}, u32[]{:S(2)}, u32[]{:S(2)}) async-start(bf16[256,4,128]{2,0,1:T(8,128)(2,1)} %pad_maximum_fusion.1), calls=%async_computation.1 | async-start | bytes 524288 | tf_op jit(solution)/shard_map/all_to_all | solution.py:88
  228.2 11.3 %all_gather.6 = s32[1,1024]{1,0:T(1,128)S(1)} all-gather(s32[1,256]{1,0:T(1,128)S(1)} %copy-done.5), channel_id=1, replica_groups=mesh['group'=2,'dp'=4,'seq'=4] {'seq'}, dimensions={1}, use_global_device_ids=true | all-gather | bytes 5120 | tf_op jit(solution)/shard_map/all_gather | solution.py:71
  239.6 1.8 copy.31
  242.2 19.8 %while.11 = (s32[]{:T(128)}, bf16[2,512,512]{2,1,0:T(8,128)(2,1)S(1)}, s32[2]{0:T(128)S(1)}, s32[1,1024]{1,0:T(1,128)S(1)}, s32[1024]{0:T(1024)S(1)}, /*index=5*...) while((s32[]{:T(128)}, ...), condition=%wide.region_4.5_spmd.clone, body=%wide.region_1.4_spmd.clone.sunk | while | flops 1103098368 | bytes 33085660 | solution.py:60
  244.3 1.9 fusion.41
  246.2 2.9 fusion.42
  249.1 2.8 divide_convert_fusion.2
  254.2 1.9 fusion.41
  256.1 2.9 fusion.42
  259.0 2.8 divide_convert_fusion.2
  262.0 26.1 %all_to_all.69 = bf16[4,256,512]{2,1,0:T(8,128)(2,1)S(1)} all-to-all(bf16[4,256,512]{2,1,0:T(8,128)(2,1)S(1)} %bitcast.127), channel_id=1, replica_groups=mesh['group'=2,'dp'=4,'seq'=4] {'seq'}, dimensions={0} | all-to-all | bytes 2097152 | tf_op jit(solution)/shard_map/all_to_all | solution.py:94
  288.7 1.4 copy.34
  (49 shorter events, 8.1 us)
Async XLA Ops:
  6.5 0.7 copy-start.4
  6.5 1.6 copy-start.1
  6.5 159.9 %all-gather.2.cloned.1.call-start = ((), (), s32[]{:S(2)}) async-start(), calls=%async_computation.4 | async-start | bytes 31457280 | tf_op jit(solution)/shard_map/all_gather | solution.py:74
  178.1 2.3 copy-start
  181.2 19.6 %slice-start = ((f32[256,3072]{1,0:T(8,128)}), f32[256,512]{1,0:T(8,128)S(1)}, s32[]{:S(2)}) async-start(f32[256,3072]{1,0:T(8,128)} %copy-done), calls=%async_computation.5 | async-start | bytes 1048576 | tf_op jit(solution)/shard_map/slice | solution.py:79
  183.2 13.9 %all-to-all-start.2 = ((bf16[256,4,128]{2,0,1:T(8,128)(2,1)}), bf16[256,4,128]{2,0,1:T(8,128)(2,1)S(1)}, u32[]{:S(2)}, u32[]{:S(2)}) async-start(bf16[256,4,128]{2,0,1:T(8,128)(2,1)} %copy_bitcast_fusion.2), calls=%async_computation.2 | async-start | bytes 524288 | tf_op jit(solution)/shard_map/all_to_all | solution.py:89
  188.1 40.1 %copy-start.5 = (s32[1,256]{1,0:T(1,128)S(1)}, s32[1,256]{1,0:T(1,128)}, u32[]{:S(2)}) copy-start(s32[1,256]{1,0:T(1,128)} %param.9) | copy-start | bytes 3076
  197.1 27.7 %copy-start.2 = (bf16[256,4,128]{2,0,1:T(8,128)(2,1)}, bf16[256,4,128]{2,0,1:T(8,128)(2,1)S(1)}, u32[]{:S(2)}) copy-start(bf16[256,4,128]{2,0,1:T(8,128)(2,1)S(1)} %all-to-all-done.2) | copy-start | bytes 786436
  197.1 27.7 %all-to-all-start = ((bf16[256,4,512]{0,2,1:T(8,128)(2,1)}), bf16[256,4,512]{0,2,1:T(8,128)(2,1)S(1)}, u32[]{:S(2)}, u32[]{:S(2)}) async-start(bf16[256,4,512]{0,2,1:T(8,128)(2,1)} %bitcast.3), calls=%async_computation | async-start | bytes 2097152 | tf_op jit(solution)/shard_map/all_to_all | solution.py:87
  224.8 17.4 %all-to-all-start.1 = ((bf16[256,4,128]{2,0,1:T(8,128)(2,1)}), bf16[256,4,128]{2,0,1:T(8,128)(2,1)S(1)}, u32[]{:S(2)}, u32[]{:S(2)}) async-start(bf16[256,4,128]{2,0,1:T(8,128)(2,1)} %pad_maximum_fusion.1), calls=%async_computation.1 | async-start | bytes 524288 | tf_op jit(solution)/shard_map/all_to_all | solution.py:88
  246.1 2.9 copy-start.3
  256.1 2.9 copy-start.3
Sparse Core Ops, SparseCore 0:
  8.9 157.4 all-gather.1
where the time goes:
time: 297 us
  waiting for transfers between devices  189 us (64%)
  blocking collectives  37.5 us (13%)
  matrix products  20.9 us (7%)
  between operations  13.6 us (5%)
  local copies, waits for them, and re-layouts  13.5 us (5%)
  starting transfers between devices  11.5 us (4%)
  other arithmetic  10.1 us (3%)
    all_gather x1, waiting for transfers between devices, local(): lax.all_gather(qkv_weight, 'dp', axis=0, tiled=True)  157 us
    all_to_all x1, blocking collectives, local(): return lax.all_to_all(back, 'seq', split_axis=0, concat_axis=2, tiled=True)  26.1 us
    all_to_all x1, waiting for transfers between devices, local(): lax.all_to_all(q_sent, 'seq', split_axis=1, concat_axis=0, tiled=True)  22.4 us
    dot_general x1, matrix products, local(): jnp.dot(normed, lax.all_gather(qkv_weight, 'dp', axis=0, tiled=True), pre...  11.6 us
    all_gather x1, blocking collectives, local(): all_docs = lax.all_gather(doc_ids, 'seq', axis=1, tiled=True)[0]  11.3 us
    all_to_all x1, waiting for transfers between devices, local(): lax.all_to_all(values, 'seq', split_axis=1, concat_axis=0, tiled=True)  7.93 us
  transfers between devices with their start and end apart: 4, of which 3 were waited for; matrix products, arithmetic and copies ran while one was open for 2% of the time, Pallas kernels for 0%

commit v1 on v0

--- a/solution.py
+++ b/solution.py
@@ -8,6 +8,36 @@
 KVH = 4
 QW = 2048
 KW = 512
+
+
+def _update_cells(x_local, where_dim, local_block):
+    r1 = x_local.shape
+    latest = x_local.reshape(
+        *r1[:where_dim], local_block, r1[where_dim] // local_block, *r1[where_dim + 1 :]
+    )
+    return jnp.moveaxis(latest, where_dim, 0)
+
+
+def move_the_routes_all(xin, pos_dim):
+    xin = jnp.moveaxis(xin, 0, pos_dim)
+    built = xin.shape
+    return xin.reshape(*built[:pos_dim], built[pos_dim] * built[pos_dim + 1], *built[pos_dim + 2 :])
+
+
+def series_solve(my_tile, group_axis, x0, arr_in):
+    q_next = lax.axis_index(group_axis)
+    reached = lax.axis_size(group_axis)
+    met_up, o_now = (reached, q_next)
+    y = _update_cells(my_tile, x0, met_up)
+    line_up = [y[o_now]]
+    for no in tuple(range(1, met_up)):
+        carry_out = y[o_now ^ no]
+        mat_out = lax.ppermute(
+            carry_out, axis_name=group_axis, perm=[(ix, ix ^ no) for ix in range(met_up)]
+        )
+        line_up.append(mat_out)
+    y = jnp.stack(line_up, 0)[o_now ^ jnp.arange(met_up)]
+    return move_the_routes_all(y, arr_in)
 
 
 def rms_norm(rows, gain):
@@ -84,7 +114,7 @@
         values = jnp.repeat(values, slots // KVH, axis=1)
     q_sent = queries.reshape(tok, count, local_q * HD)
     q_got, k_got, v_got = (
-        lax.all_to_all(q_sent, "seq", split_axis=1, concat_axis=0, tiled=True),
+        series_solve(q_sent, group_axis="seq", x0=1, arr_in=0),
         lax.all_to_all(keys, "seq", split_axis=1, concat_axis=0, tiled=True),
         lax.all_to_all(values, "seq", split_axis=1, concat_axis=0, tiled=True),
     )

time: 297 us -> 286 us (0.963)
  waiting for transfers between devices: 189 us -> 158 us
  blocking collectives: 37.5 us -> 51.5 us
    all_to_all x1 -> x0, waiting for transfers between devices: 22.4 us -> none  [local(): lax.all_to_all(q_sent, 'seq', split_axis=1, concat_axis=0, tiled=True)]
    all_to_all x1, waiting for transfers between devices: 7.93 us -> 0.01 us  [local(): lax.all_to_all(values, 'seq', split_axis=1, concat_axis=0, tiled=True)]
    all_to_all x1, blocking collectives: 26.1 us -> 33.5 us  [local(): return lax.all_to_all(back, 'seq', split_axis=0, concat_axis=2, tiled=True)]
    all_gather x1, blocking collectives: 11.3 us -> 18 us  [local(): all_docs = lax.all_gather(doc_ids, 'seq', axis=1, tiled=True)[0]]
    ppermute x0 -> x3, starting transfers between devices: none -> 4.53 us  [series_solve(): lax.ppermute(carry_out, axis_name=group_axis, perm=[(ix, ix ^ no) for ix...]
    all_to_all x1 -> x0, starting transfers between devices: 3.52 us -> none  [local(): lax.all_to_all(q_sent, 'seq', split_axis=1, concat_axis=0, tiled=True)]
  transfers between devices with their start and end apart: 4 -> 6, of which waited for: 3 -> 2; matrix products, arithmetic and copies ran while one was open for 2% -> 4% of each run, Pallas kernels for 0% -> 0%
where the time goes in v1:
time: 286 us; the launch traced here: 285 us
  waiting for transfers between devices  158 us (55%)
  blocking collectives  51.5 us (18%)
  matrix products  22.7 us (8%)
  starting transfers between devices  14.2 us (5%)
  between operations  13.6 us (5%)
  local copies, waits for them, and re-layouts  12.3 us (4%)
  other arithmetic  11.8 us (4%)
    all_gather x1, waiting for transfers between devices, local(): lax.all_gather(qkv_weight, 'dp', axis=0, tiled=True)  157 us
    all_to_all x1, blocking collectives, local(): return lax.all_to_all(back, 'seq', split_axis=0, concat_axis=2, tiled=True)  33.5 us
    all_gather x1, blocking collectives, local(): all_docs = lax.all_gather(doc_ids, 'seq', axis=1, tiled=True)[0]  18 us
    dot_general x1, matrix products, local(): jnp.dot(normed, lax.all_gather(qkv_weight, 'dp', axis=0, tiled=True), pre...  11.6 us
    dot_general x2, matrix products, one_block(): jnp.einsum('kgqt,tkd->qkgd', weights, values, preferred_element_type=jnp....  7.38 us
    reduce_sum x2, other arithmetic, one_block(): total = jnp.sum(expo, axis=-1)  5.85 us
  transfers between devices with their start and end apart: 6, of which 2 were waited for; matrix products, arithmetic and copies ran while one was open for 4% of the time, Pallas kernels for 0%

profile of v1, /device:TPU:0, one launch (start us, length us, event | category | flops | bytes accessed | tf_op | source)
XLA Modules:
  0.0 285.3 jit_solution(10566376514191405454)
XLA Ops:
  7.6 0.7 copy.32
  8.4 0.8 copy.34
  9.6 156.8 %all-gather.2.cloned.1.call-done = bf16[4096,3072]{1,0:T(8,128)(2,1)} async-done(((bf16[1024,3072]{1,0:T(8,128)(2,1)}), bf16[4096,3072]{1,0:T(8,128)(2,1)}) %all-gather.2.cloned.1.call-update) | async-done | bytes 25165840 | tf_op jit(solution)/shard_map/all_gather | solution.py:104
  166.4 11.6 %fusion.24 = f32[256,3072]{1,0:T(8,128)S(1)} fusion(bf16[4096,3072]{1,0:T(8,128)(2,1)} %all-gather.2.cloned.1.call-done, bf16[1,256,4096]{2,1,0:T(8,128)(2,1)S(1)} %copy-done, f32[4096]{0:T(1024)S(1)} %convert_element_type.53, f32[256]{0:T(256)S(1)} %add_rsqrt_fusion), kind=kOutput, calls=%fused_computation.29 | convolution fusion | flops 6446645248 | bytes 30426112 | tf_op jit(solution)/shard_map/dot_general | solution.py:102
  178.1 0.7 copy_bitcast_fusion.2
  179.0 4.6 %all-to-all-start.1 = ((bf16[256,4,128]{2,0,1:T(8,128)(2,1)}), bf16[256,4,128]{2,0,1:T(8,128)(2,1)S(1)}, u32[]{:S(2)}, u32[]{:S(2)}) async-start(bf16[256,4,128]{2,0,1:T(8,128)(2,1)} %copy_bitcast_fusion.2), calls=%async_computation.1 | async-start | bytes 524288 | tf_op jit(solution)/shard_map/all_to_all | solution.py:119
  183.6 1.8 copy.41
  185.5 1.9 subtract_convert_fusion
  188.2 2.1 collective-permute-start
  190.3 2.4 collective-permute-start.1
  193.2 0.9 pad_maximum_fusion.1
  194.1 5.0 %all-to-all-start = ((bf16[256,4,128]{2,0,1:T(8,128)(2,1)}), bf16[256,4,128]{2,0,1:T(8,128)(2,1)S(1)}, u32[]{:S(2)}, u32[]{:S(2)}) async-start(bf16[256,4,128]{2,0,1:T(8,128)(2,1)} %pad_maximum_fusion.1), calls=%async_computation | async-start | bytes 524288 | tf_op jit(solution)/shard_map/all_to_all | solution.py:118
  199.1 18.0 %all_gather.6 = s32[1,1024]{1,0:T(1,128)S(1)} all-gather(s32[1,256]{1,0:T(1,128)S(1)} %copy-done.5), channel_id=1, replica_groups=mesh['group'=2,'dp'=4,'seq'=4] {'seq'}, dimensions={1}, use_global_device_ids=true | all-gather | bytes 5120 | tf_op jit(solution)/shard_map/all_gather | solution.py:101
  217.2 1.2 maximum_bitcast_fusion
  219.3 1.8 copy.37
  221.3 21.6 %while.11 = (s32[]{:T(128)}, bf16[2,512,512]{2,1,0:T(8,128)(2,1)S(1)}, s32[2]{0:T(128)S(1)}, s32[1,1024]{1,0:T(1,128)S(1)}, s32[1024]{0:T(1024)S(1)}, /*index=5*...) while((s32[]{:T(128)}, ...), condition=%wide.region_4.5_spmd.clone, body=%wide.region_1.4_spmd.clone.sunk | while | flops 1103098368 | bytes 32037064 | solution.py:90
  223.3 1.9 fusion.42
  225.2 2.9 %fusion.43 = f32[4,512]{1,0:T(4,128)S(1)} fusion(f32[512,4,1024]{2,0,1:T(8,128)S(1)} %get-tuple-element.176, f32[4,512]{1,0:T(4,128)S(1)} %get-tuple-element.177, pred[512,1024]{1,0:T(8,128)(4,1)S(1)} %fusion.41), kind=kLoop, calls=%fused_computation.5.clone.1 | loop fusion | flops 10483712 | bytes 8929280 | tf_op jit(solution)/shard_map/while/body/eval_jaxpr/reduce_sum | solution.py:84
  228.1 3.7 %divide_convert_fusion.2 = bf16[512,1,4,128]{0,3,2,1:T(8,128)(2,1)S(1)} fusion(f32[512,4,1024]{2,0,1:T(8,128)S(1)} %get-tuple-element.176, f32[4,512]{1,0:T(4,128)S(1)} %get-tuple-element.177, pred[512,1024]{1,0:T(8,128)(4,1)S(1)} %fusion.41, f32[512,4]{0,1:T(4,128)S(1)} %bitcast.140, bf16[1024,1,128]{0,2,1:T(8,128)(2,1)} %get-tuple-element.209), kind=kOutput, calls=%fused_computation.13.clone.1 | convolution fusion | flops 547880960 | bytes 9715712 | tf_op jit(solution)/shard_map/while/body/eval_jaxpr/kgqt,tkd->qkgd/dot_general | solution.py:86
  234.1 1.9 fusion.42
  236.0 2.9 %fusion.43 = f32[4,512]{1,0:T(4,128)S(1)} fusion(f32[512,4,1024]{2,0,1:T(8,128)S(1)} %get-tuple-element.176, f32[4,512]{1,0:T(4,128)S(1)} %get-tuple-element.177, pred[512,1024]{1,0:T(8,128)(4,1)S(1)} %fusion.41), kind=kLoop, calls=%fused_computation.5.clone.1 | loop fusion | flops 10483712 | bytes 8929280 | tf_op jit(solution)/shard_map/while/body/eval_jaxpr/reduce_sum | solution.py:84
  238.9 3.7 %divide_convert_fusion.2 = bf16[512,1,4,128]{0,3,2,1:T(8,128)(2,1)S(1)} fusion(f32[512,4,1024]{2,0,1:T(8,128)S(1)} %get-tuple-element.176, f32[4,512]{1,0:T(4,128)S(1)} %get-tuple-element.177, pred[512,1024]{1,0:T(8,128)(4,1)S(1)} %fusion.41, f32[512,4]{0,1:T(4,128)S(1)} %bitcast.140, bf16[1024,1,128]{0,2,1:T(8,128)(2,1)} %get-tuple-element.209), kind=kOutput, calls=%fused_computation.13.clone.1 | convolution fusion | flops 547880960 | bytes 9715712 | tf_op jit(solution)/shard_map/while/body/eval_jaxpr/kgqt,tkd->qkgd/dot_general | solution.py:86
  242.9 33.5 %all_to_all.54 = bf16[4,256,512]{2,1,0:T(8,128)(2,1)S(1)} all-to-all(bf16[4,256,512]{2,1,0:T(8,128)(2,1)S(1)} %bitcast.131), channel_id=1, replica_groups=mesh['group'=2,'dp'=4,'seq'=4] {'seq'}, dimensions={0} | all-to-all | bytes 2097152 | tf_op jit(solution)/shard_map/all_to_all | solution.py:124
  277.0 1.4 copy.40
  (58 shorter events, 8.0 us)
Async XLA Ops:
  6.5 0.7 copy-start.4
  6.5 2.6 copy-start
  6.5 159.9 %all-gather.2.cloned.1.call-start = ((), (), s32[]{:S(2)}) async-start(), calls=%async_computation.3 | async-start | bytes 31457280 | tf_op jit(solution)/shard_map/all_gather | solution.py:104
  179.0 15.1 %all-to-all-start.1 = ((bf16[256,4,128]{2,0,1:T(8,128)(2,1)}), bf16[256,4,128]{2,0,1:T(8,128)(2,1)S(1)}, u32[]{:S(2)}, u32[]{:S(2)}) async-start(bf16[256,4,128]{2,0,1:T(8,128)(2,1)} %copy_bitcast_fusion.2), calls=%async_computation.1 | async-start | bytes 524288 | tf_op jit(solution)/shard_map/all_to_all | solution.py:119
  185.5 7.6 %copy-start.2 = (f32[256,64]{1,0:T(8,128)S(1)}, f32[256,64]{1,0:T(8,128)}, u32[]{:S(2)}) copy-start(f32[256,64]{1,0:T(8,128)} %copy.32) | copy-start | bytes 196612
  185.5 7.6 %copy-start.3 = (f32[256,64]{1,0:T(8,128)S(1)}, f32[256,64]{1,0:T(8,128)}, u32[]{:S(2)}) copy-start(f32[256,64]{1,0:T(8,128)} %copy.34) | copy-start | bytes 196612
  187.4 11.7 %copy-start.5 = (s32[1,256]{1,0:T(1,128)S(1)}, s32[1,256]{1,0:T(1,128)}, u32[]{:S(2)}) copy-start(s32[1,256]{1,0:T(1,128)} %param.9) | copy-start | bytes 3076
  188.2 29.0 %collective-permute-start = (bf16[256,1,512]{2,0,1:T(8,128)(2,1)S(1)}, bf16[256,1,512]{2,0,1:T(8,128)(2,1)S(1)}, u32[]{:S(2)}, u32[]{:S(2)}) collective-permute-start(bf16[256,1,512]{2,0,1:T(8,128)(2,1)S(1)} %bitcast.138), channel_id=1, source_target_pairs={{0,1},{1,0},{2,3},{3,2},{4,5},{5,4},{6,7},{7,6},{8,9},{9,8},{10,11... | collective-permute-start | bytes 786440 | tf_op jit(solution)/shard_map/ppermute | solution.py:35
  190.3 27.0 %collective-permute-start.1 = (bf16[256,1,512]{2,0,1:T(8,128)(2,1)S(1)}, bf16[256,1,512]{2,0,1:T(8,128)(2,1)}, u32[]{:S(2)}, u32[]{:S(2)}) collective-permute-start(bf16[256,1,512]{2,0,1:T(8,128)(2,1)S(1)} %bitcast.137), channel_id=1, source_target_pairs={{0,2},{1,3},{2,0},{3,1},{4,6},{5,7},{6,4},{7,5},{8,10},{9,11},{10,... | collective-permute-start | bytes 786440 | tf_op jit(solution)/shard_map/ppermute | solution.py:35
  192.6 24.6 %collective-permute-start.2 = (bf16[256,1,512]{2,0,1:T(8,128)(2,1)S(1)}, bf16[256,1,512]{2,0,1:T(8,128)(2,1)}, u32[]{:S(2)}, u32[]{:S(2)}) collective-permute-start(bf16[256,1,512]{2,0,1:T(8,128)(2,1)S(1)} %bitcast.136), channel_id=1, source_target_pairs={{0,3},{1,2},{2,1},{3,0},{4,7},{5,6},{6,5},{7,4},{8,11},{9,10},{10,... | collective-permute-start | bytes 786440 | tf_op jit(solution)/shard_map/ppermute | solution.py:35
  194.1 23.2 %copy-start.1 = (bf16[256,4,128]{2,0,1:T(8,128)(2,1)}, bf16[256,4,128]{2,0,1:T(8,128)(2,1)S(1)}, u32[]{:S(2)}) copy-start(bf16[256,4,128]{2,0,1:T(8,128)(2,1)S(1)} %all-to-all-done.1) | copy-start | bytes 786436
  194.1 27.2 %all-to-all-start = ((bf16[256,4,128]{2,0,1:T(8,128)(2,1)}), bf16[256,4,128]{2,0,1:T(8,128)(2,1)S(1)}, u32[]{:S(2)}, u32[]{:S(2)}) async-start(bf16[256,4,128]{2,0,1:T(8,128)(2,1)} %pad_maximum_fusion.1), calls=%async_computation | async-start | bytes 524288 | tf_op jit(solution)/shard_map/all_to_all | solution.py:118
Sparse Core Ops, SparseCore 0:
  8.9 157.4 all-gather.1
